TPU v7x, 32 devices: a whole 2x2x4 slice. The times are simulated.
32 devices in a mesh: dp: 8 (over z, x), mp: 4 (over y, core).
Axes of the slice: x: 2, y: 2, z: 4, core: 2. Of those that a mesh axis runs over, the one named last changes fastest.
Arguments:
- hidden_in: float32 [4096, 1024], P(('dp', 'mp')), may hold values from -6 to 6
- seg_ids: int32 [8, 512], P('dp'), may hold values from 0 to 7, never falling along the last dimension, each value on 1 to 128 neighbouring positions
- cotangent: float32 [4096, 1024], P(('dp', 'mp')), may hold values from -6 to 6
- w_qkv: float32 [2, 1024, 3072], P(None, 'dp', 'mp'), as said below
- w_dense: float32 [2, 1024, 1024], P(None, 'dp', 'mp'), may hold values from -0.5 to 0.5
- w_up: float32 [2, 1024, 4096], P(None, 'dp', 'mp'), may hold values from -0.1875 to 0.1875
- w_down: float32 [2, 1024, 4096], P(None, 'dp', 'mp'), may hold values from -0.09375 to 0.09375
- norm_gain: float32 [2, 2, 1024], replicated, may hold values from 0.5 to 1.5
- norm_bias: float32 [2, 2, 1024], replicated, may hold values from -2 to 2
- qkv_bias: float32 [2, 3072], replicated, may hold values from -2 to 2
- out_bias: float32 [2, 2, 1024], replicated, may hold values from -2 to 2
- up_bias: float32 [2, 4096], replicated, may hold values from -2 to 2
- qkv_moments: float32 [2, 2, 1024, 3072], P(None, None, 'dp', 'mp'), as said below
- dense_moments: float32 [2, 2, 1024, 1024], P(None, None, 'dp', 'mp'), as said below
- up_moments: float32 [2, 2, 1024, 4096], P(None, None, 'dp', 'mp'), as said below
- down_moments: float32 [2, 2, 1024, 4096], P(None, None, 'dp', 'mp'), as said below
- gain_moments: float32 [2, 2, 2, 1024], replicated, as said below
- nbias_moments: float32 [2, 2, 2, 1024], replicated, as said below
- qbias_moments: float32 [2, 2, 3072], replicated, as said below
- obias_moments: float32 [2, 2, 2, 1024], replicated, as said below
- ubias_moments: float32 [2, 2, 4096], replicated, as said below
Outputs:
- hidden_out: float32 [4096, 1024], P(('dp', 'mp'))
- hidden_grad: float32 [4096, 1024], P(('dp', 'mp'))
- qkv_grad: float32 [2, 1024, 3072], P(None, 'dp', 'mp')
- dense_grad: float32 [2, 1024, 1024], P(None, 'dp', 'mp')
- up_grad: float32 [2, 1024, 4096], P(None, 'dp', 'mp')
- down_grad: float32 [2, 1024, 4096], P(None, 'dp', 'mp')
- gain_grad: float32 [2, 2, 1024], replicated
- nbias_grad: float32 [2, 2, 1024], replicated
- qbias_grad: float32 [2, 3072], replicated
- obias_grad: float32 [2, 2, 1024], replicated
- ubias_grad: float32 [2, 4096], replicated
- qkv_new: float32 [2, 1024, 3072], P(None, 'dp', 'mp')
- dense_new: float32 [2, 1024, 1024], P(None, 'dp', 'mp')
- up_new: float32 [2, 1024, 4096], P(None, 'dp', 'mp')
- down_new: float32 [2, 1024, 4096], P(None, 'dp', 'mp')
- gain_new: float32 [2, 2, 1024], replicated
- nbias_new: float32 [2, 2, 1024], replicated
- qbias_new: float32 [2, 3072], replicated
- obias_new: float32 [2, 2, 1024], replicated
- ubias_new: float32 [2, 4096], replicated
- qkv_states: float32 [2, 2, 1024, 3072], P(None, None, 'dp', 'mp')
- dense_states: float32 [2, 2, 1024, 1024], P(None, None, 'dp', 'mp')
- up_states: float32 [2, 2, 1024, 4096], P(None, None, 'dp', 'mp')
- down_states: float32 [2, 2, 1024, 4096], P(None, None, 'dp', 'mp')
- gain_states: float32 [2, 2, 2, 1024], replicated
- nbias_states: float32 [2, 2, 2, 1024], replicated
- qbias_states: float32 [2, 2, 3072], replicated
- obias_states: float32 [2, 2, 2, 1024], replicated
- ubias_states: float32 [2, 2, 4096], replicated
Inputs may be any that keep to these rules, and one draw needn't show every extreme that they name: `w_qkv`: columns of each head hold its query, then its key, then its value. `qkv_moments`: the first slice holds first moments, the second slice positive second moments. `dense_moments`: the first slice holds first moments, the second slice positive second moments. `up_moments`: the first slice holds first moments, the second slice positive second moments. `down_moments`: the first slice holds first moments, the second slice positive second moments. `gain_moments`: the first slice holds first moments, the second slice positive second moments. `nbias_moments`: the first slice holds first moments, the second slice positive second moments. `qbias_moments`: the first slice holds first moments, the second slice positive second moments. `obias_moments`: the first slice holds first moments, the second slice positive second moments. `ubias_moments`: the first slice holds first moments, the second slice positive second moments.
All inputs are finite; a program needn't handle non-finite values.
Results may differ from a plain program's by a relative error of at most 0.024.
Values may be sent and summed in bfloat16 or wider, within the bound.
A program may use at most 128 MiB of HBM per device.

v0:
```python
import jax
import jax.numpy as jnp
from jax import lax
from jax.sharding import PartitionSpec as P

HEADS = 16
HD = 64


norm_eps = 1e-05
beta_first = 0.9
beta_second = 0.999
adam_eps = 1e-08
learn_rate = 0.01
weight_decay = 0.1
adam_step = 3.0
gelu_scale = 0.7978845608028654
gelu_cubic = 0.044715
contract_cols = (((1,), (1,)), ((), ()))
contract_rows = (((0,), (0,)), ((), ()))


def layer_norm(values, gain_vec, shift_vec):
    centered = values - jnp.mean(values, axis=-1, keepdims=True)
    inv_std = lax.rsqrt(jnp.mean(centered * centered, axis=-1, keepdims=True) + norm_eps)
    normed = centered * inv_std
    return (normed * gain_vec + shift_vec, normed, inv_std)


def norm_backward(upstream, normed, inv_std, gain_vec):
    scaled = upstream * gain_vec
    mean_one = jnp.mean(scaled, axis=-1, keepdims=True)
    mean_two = jnp.mean(scaled * normed, axis=-1, keepdims=True)
    return inv_std * (scaled - mean_one - normed * mean_two)


def gelu_parts(pre_act):
    inner_arg = gelu_scale * (pre_act + gelu_cubic * pre_act * pre_act * pre_act)
    tangent = jnp.tanh(inner_arg)
    result = 0.5 * pre_act * (1.0 + tangent)
    deriv = 0.5 * (1.0 + tangent) + 0.5 * pre_act * (1.0 - tangent * tangent) * gelu_scale * (
        1.0 + 3.0 * gelu_cubic * pre_act * pre_act
    )
    return (result, deriv)


def split_heads(joined):
    row_count = joined.shape[0]
    head_count = joined.shape[1] // (3 * HD)
    pieces = joined.reshape(row_count, head_count, 3, HD)
    return (pieces[:, :, 0], pieces[:, :, 1], pieces[:, :, 2])


def masked_scores(queries, key_rows, seg_row, slopes):
    row_count = queries.shape[0]
    scores = jnp.einsum(
        "qhe,khe->hqk", queries, key_rows, preferred_element_type=jnp.float32
    ) * HD ** (-0.5)
    position = jnp.arange(row_count, dtype=jnp.int32)
    offset = (position[None, :] - position[:, None]).astype(jnp.float32)
    scores = scores + slopes[:, None, None] * offset[None]
    allowed = (position[None, :] <= position[:, None]) & (seg_row[:, None] == seg_row[None, :])
    return jnp.where(allowed[None], scores, -jnp.inf)


def attend(joined, seg_row, slopes):
    queries, key_rows, value_rows = split_heads(joined)
    scores = masked_scores(queries, key_rows, seg_row, slopes)
    highest = jnp.max(scores, axis=-1, keepdims=True)
    log_total = highest + jnp.log(jnp.sum(jnp.exp(scores - highest), axis=-1, keepdims=True))
    weights = jnp.exp(scores - log_total).astype(jnp.bfloat16)
    mixed = jnp.einsum("hqk,khe->qhe", weights, value_rows, preferred_element_type=jnp.float32)
    return (mixed.astype(jnp.bfloat16).reshape(joined.shape[0], -1), log_total)


def attend_backward(grad_mix, joined, mixed, log_total, seg_row, slopes):
    queries, key_rows, value_rows = split_heads(joined)
    row_count = joined.shape[0]
    head_count = queries.shape[1]
    scores = masked_scores(queries, key_rows, seg_row, slopes)
    probs = jnp.exp(scores - log_total)
    weights = probs.astype(jnp.bfloat16)
    grad_heads = grad_mix.reshape(row_count, head_count, HD)
    grad_values = jnp.einsum(
        "hqk,qhe->khe", weights, grad_heads, preferred_element_type=jnp.float32
    )
    grad_probs = jnp.einsum(
        "qhe,khe->hqk", grad_heads, value_rows, preferred_element_type=jnp.float32
    )
    delta = jnp.sum(
        grad_heads.astype(jnp.float32)
        * mixed.reshape(row_count, head_count, HD).astype(jnp.float32),
        axis=-1,
    )
    grad_scores = (probs * (grad_probs - jnp.transpose(delta)[:, :, None])).astype(jnp.bfloat16)
    grad_queries = jnp.einsum(
        "hqk,khe->qhe", grad_scores, key_rows, preferred_element_type=jnp.float32
    ) * HD ** (-0.5)
    grad_keys = jnp.einsum(
        "hqk,qhe->khe", grad_scores, queries, preferred_element_type=jnp.float32
    ) * HD ** (-0.5)
    return jnp.stack([grad_queries, grad_keys, grad_values], axis=2).reshape(row_count, -1)


def gather_norm(normed_rows):
    return lax.all_gather(normed_rows, "mp", axis=0, tiled=True)


def gather_cot(grad_rows):
    return lax.all_gather(grad_rows, "mp", axis=0, tiled=True)


def project_sum(left, right):

    def term(row_start, row_count):
        return lax.dot_general(left, right, contract_cols, preferred_element_type=jnp.float32)

    return lax.psum_scatter(
        term(jnp.int32(0), left.shape[0] // lax.axis_size("mp") * lax.axis_size("mp")),
        "mp",
        scatter_dimension=0,
        tiled=True,
    )


def project_back(left, right):

    def term(row_start, row_count):
        return lax.dot_general(left, right, contract_cols, preferred_element_type=jnp.float32)

    return lax.psum_scatter(
        term(jnp.int32(0), left.shape[0] // lax.axis_size("mp") * lax.axis_size("mp")),
        "mp",
        scatter_dimension=0,
        tiled=True,
    )


def local_parts(weight_pairs):
    return tuple(
        (
            lax.dot_general(left_op, right_op, contract_rows, preferred_element_type=jnp.float32)
            for left_op, right_op in weight_pairs
        )
    )


def forward_layer(stream_in, seg_row, matrices, vectors, slopes):
    w_joined, w_proj, w_expand, w_shrink = matrices
    gain_vec, shift_vec, joined_bias, out_shift, expand_bias = vectors
    normed_out, normed_one, inv_one = layer_norm(stream_in, gain_vec[0], shift_vec[0])
    rows_one = gather_norm(normed_out.astype(jnp.bfloat16))
    joined = (jnp.dot(rows_one, w_joined, preferred_element_type=jnp.float32) + joined_bias).astype(
        jnp.bfloat16
    )
    mixed, log_total = attend(joined, seg_row, slopes)
    middle = stream_in + project_sum(mixed, w_proj) + out_shift[0]
    normed_mid, normed_two, inv_two = layer_norm(middle, gain_vec[1], shift_vec[1])
    rows_two = gather_norm(normed_mid.astype(jnp.bfloat16))
    pre_act = jnp.dot(rows_two, w_expand, preferred_element_type=jnp.float32) + expand_bias
    activated, deriv = gelu_parts(pre_act)
    hidden_act = activated.astype(jnp.bfloat16)
    result = middle + project_sum(hidden_act, w_shrink) + out_shift[1]
    return (
        result,
        (
            normed_one,
            inv_one,
            rows_one,
            joined,
            mixed,
            log_total,
            normed_two,
            inv_two,
            rows_two,
            deriv,
            hidden_act,
        ),
    )


def backward_layer(upstream, seg_row, matrices, vectors, saved, slopes):
    w_joined, w_proj, w_expand, w_shrink = matrices
    gain_vec, shift_vec, joined_bias, out_shift, expand_bias = vectors
    (
        normed_one,
        inv_one,
        rows_one,
        joined,
        mixed,
        log_total,
        normed_two,
        inv_two,
        rows_two,
        deriv,
        hidden_act,
    ) = saved
    grad_rows = gather_cot(upstream.astype(jnp.bfloat16))
    grad_hidden = jnp.dot(grad_rows, w_shrink, preferred_element_type=jnp.float32)
    grad_pre = grad_hidden * deriv
    pre_rounded = grad_pre.astype(jnp.bfloat16)
    grad_norm_two = project_back(pre_rounded, w_expand)
    gain_two = jnp.sum(grad_norm_two * normed_two, axis=0)
    shift_two = jnp.sum(grad_norm_two, axis=0)
    middle = upstream + norm_backward(grad_norm_two, normed_two, inv_two, gain_vec[1])
    grad_rows_one = gather_cot(middle.astype(jnp.bfloat16))
    grad_mixed = jnp.dot(grad_rows_one, w_proj, preferred_element_type=jnp.float32).astype(
        jnp.bfloat16
    )
    grad_joined = attend_backward(grad_mixed, joined, mixed, log_total, seg_row, slopes)
    joined_rounded = grad_joined.astype(jnp.bfloat16)
    grad_norm_one = project_back(joined_rounded, w_joined)
    gain_one = jnp.sum(grad_norm_one * normed_one, axis=0)
    shift_one = jnp.sum(grad_norm_one, axis=0)
    grad_below = middle + norm_backward(grad_norm_one, normed_one, inv_one, gain_vec[0])
    weight_pairs = (
        (rows_one, joined_rounded),
        (grad_rows_one, mixed),
        (rows_two, pre_rounded),
        (grad_rows, hidden_act),
    )
    small_grads = (
        jnp.stack([gain_one, gain_two]),
        jnp.stack([shift_one, shift_two]),
        jnp.sum(grad_joined, axis=0),
        jnp.stack([jnp.sum(middle, axis=0), jnp.sum(upstream, axis=0)]),
        jnp.sum(grad_pre, axis=0),
    )
    return (grad_below, weight_pairs, small_grads)


def adamw(weight, gradient, moments, decay):
    first = beta_first * moments[0] + (1.0 - beta_first) * gradient
    second = beta_second * moments[1] + (1.0 - beta_second) * gradient * gradient
    first_hat = first / (1.0 - beta_first**adam_step)
    second_hat = second / (1.0 - beta_second**adam_step)
    updated = weight - learn_rate * (first_hat / (jnp.sqrt(second_hat) + adam_eps) + decay * weight)
    return (updated, jnp.stack([first, second]))


def per_device(
    hidden_in,
    seg_ids,
    cotangent,
    w_qkv,
    w_dense,
    w_up,
    w_down,
    norm_gain,
    norm_bias,
    qkv_bias,
    out_bias,
    up_bias,
    qkv_moments,
    dense_moments,
    up_moments,
    down_moments,
    gain_moments,
    nbias_moments,
    qbias_moments,
    obias_moments,
    ubias_moments,
):
    mp_index = lax.axis_index("mp")
    mp_count = lax.axis_size("mp")
    head_local = HEADS // mp_count
    qkv_cols = w_qkv.shape[2]
    up_cols = w_up.shape[2]
    layer_count = w_qkv.shape[0]
    all_slopes = 2.0 ** (-8.0 * jnp.arange(1, HEADS + 1, dtype=jnp.float32) / HEADS)
    slopes = lax.dynamic_slice_in_dim(all_slopes, mp_index * head_local, head_local)
    seg_row = seg_ids[0]
    qkv_local = lax.dynamic_slice_in_dim(qkv_bias, mp_index * qkv_cols, qkv_cols, axis=1)
    up_local = lax.dynamic_slice_in_dim(up_bias, mp_index * up_cols, up_cols, axis=1)

    def vectors_of(layer_idx):
        return (
            norm_gain[layer_idx],
            norm_bias[layer_idx],
            qkv_local[layer_idx],
            out_bias[layer_idx],
            up_local[layer_idx],
        )

    stream = hidden_in
    kept_mats = []
    kept_acts = []
    for layer_idx in range(layer_count):
        matrices = (
            lax.all_gather(w_qkv[layer_idx].astype(jnp.bfloat16), "dp", axis=0, tiled=True),
            lax.all_gather(w_dense[layer_idx].astype(jnp.bfloat16), "dp", axis=0, tiled=True),
            lax.all_gather(w_up[layer_idx].astype(jnp.bfloat16), "dp", axis=0, tiled=True),
            lax.all_gather(w_down[layer_idx].astype(jnp.bfloat16), "dp", axis=0, tiled=True),
        )
        stream, saved = forward_layer(stream, seg_row, matrices, vectors_of(layer_idx), slopes)
        kept_mats.append(matrices)
        kept_acts.append(saved)
    upstream = cotangent
    reduced = [None] * layer_count
    small_parts = [None] * layer_count
    for layer_idx in reversed(range(layer_count)):
        matrices = (
            lax.all_gather(w_qkv[layer_idx].astype(jnp.bfloat16), "dp", axis=0, tiled=True),
            lax.all_gather(w_dense[layer_idx].astype(jnp.bfloat16), "dp", axis=0, tiled=True),
            lax.all_gather(w_up[layer_idx].astype(jnp.bfloat16), "dp", axis=0, tiled=True),
            lax.all_gather(w_down[layer_idx].astype(jnp.bfloat16), "dp", axis=0, tiled=True),
        )
        upstream, weight_pairs, small_grads = backward_layer(
            upstream, seg_row, matrices, vectors_of(layer_idx), kept_acts[layer_idx], slopes
        )
        weight_grads = local_parts(weight_pairs)
        reduced[layer_idx] = (
            lax.psum_scatter(
                weight_grads[0].astype(jnp.bfloat16), "dp", scatter_dimension=0, tiled=True
            ).astype(jnp.float32),
            lax.psum_scatter(
                weight_grads[1].astype(jnp.bfloat16), "dp", scatter_dimension=0, tiled=True
            ).astype(jnp.float32),
            lax.psum_scatter(
                weight_grads[2].astype(jnp.bfloat16), "dp", scatter_dimension=0, tiled=True
            ).astype(jnp.float32),
            lax.psum_scatter(
                weight_grads[3].astype(jnp.bfloat16), "dp", scatter_dimension=0, tiled=True
            ).astype(jnp.float32),
        )
        small_parts[layer_idx] = small_grads
    qkv_grad = jnp.stack([reduced[layer_idx][0] for layer_idx in range(layer_count)])
    dense_grad = jnp.stack([reduced[layer_idx][1] for layer_idx in range(layer_count)])
    up_grad = jnp.stack([reduced[layer_idx][2] for layer_idx in range(layer_count)])
    down_grad = jnp.stack([reduced[layer_idx][3] for layer_idx in range(layer_count)])

    def widen(small_piece, total_len):
        return lax.dynamic_update_slice_in_dim(
            jnp.zeros((total_len,), jnp.float32), small_piece, mp_index * small_piece.shape[0], 0
        )

    gain_part = jnp.stack([small_parts[layer_idx][0] for layer_idx in range(layer_count)])
    nbias_part = jnp.stack([small_parts[layer_idx][1] for layer_idx in range(layer_count)])
    qbias_part = jnp.stack(
        [widen(small_parts[layer_idx][2], qkv_bias.shape[1]) for layer_idx in range(layer_count)]
    )
    obias_part = jnp.stack([small_parts[layer_idx][3] for layer_idx in range(layer_count)])
    ubias_part = jnp.stack(
        [widen(small_parts[layer_idx][4], up_bias.shape[1]) for layer_idx in range(layer_count)]
    )
    gain_grad, nbias_grad, qbias_grad, obias_grad, ubias_grad = lax.psum(
        (gain_part, nbias_part, qbias_part, obias_part, ubias_part), ("dp", "mp")
    )
    qkv_new, qkv_states = adamw(w_qkv, qkv_grad, qkv_moments, weight_decay)
    dense_new, dense_states = adamw(w_dense, dense_grad, dense_moments, weight_decay)
    up_new, up_states = adamw(w_up, up_grad, up_moments, weight_decay)
    down_new, down_states = adamw(w_down, down_grad, down_moments, weight_decay)
    gain_new, gain_states = adamw(norm_gain, gain_grad, gain_moments, 0.0)
    nbias_new, nbias_states = adamw(norm_bias, nbias_grad, nbias_moments, 0.0)
    qbias_new, qbias_states = adamw(qkv_bias, qbias_grad, qbias_moments, 0.0)
    obias_new, obias_states = adamw(out_bias, obias_grad, obias_moments, 0.0)
    ubias_new, ubias_states = adamw(up_bias, ubias_grad, ubias_moments, 0.0)
    return (
        stream,
        upstream,
        qkv_grad,
        dense_grad,
        up_grad,
        down_grad,
        gain_grad,
        nbias_grad,
        qbias_grad,
        obias_grad,
        ubias_grad,
        qkv_new,
        dense_new,
        up_new,
        down_new,
        gain_new,
        nbias_new,
        qbias_new,
        obias_new,
        ubias_new,
        qkv_states,
        dense_states,
        up_states,
        down_states,
        gain_states,
        nbias_states,
        qbias_states,
        obias_states,
        ubias_states,
    )


def solution(mesh):
    return jax.shard_map(
        per_device,
        mesh=mesh,
        in_specs=(
            P(("dp", "mp"), None),
            P("dp", None),
            P(("dp", "mp"), None),
            P(None, "dp", "mp"),
            P(None, "dp", "mp"),
            P(None, "dp", "mp"),
            P(None, "dp", "mp"),
            P(),
            P(),
            P(),
            P(),
            P(),
            P(None, None, "dp", "mp"),
            P(None, None, "dp", "mp"),
            P(None, None, "dp", "mp"),
            P(None, None, "dp", "mp"),
            P(),
            P(),
            P(),
            P(),
            P(),
        ),
        out_specs=(
            P(("dp", "mp"), None),
            P(("dp", "mp"), None),
            P(None, "dp", "mp"),
            P(None, "dp", "mp"),
            P(None, "dp", "mp"),
            P(None, "dp", "mp"),
            P(),
            P(),
            P(),
            P(),
            P(),
            P(None, "dp", "mp"),
            P(None, "dp", "mp"),
            P(None, "dp", "mp"),
            P(None, "dp", "mp"),
            P(),
            P(),
            P(),
            P(),
            P(),
            P(None, None, "dp", "mp"),
            P(None, None, "dp", "mp"),
            P(None, None, "dp", "mp"),
            P(None, None, "dp", "mp"),
            P(),
            P(),
            P(),
            P(),
            P(),
        ),
        check_vma=False,
    )
```

profile of v0, /device:TPU:0, one launch (start us, length us, event | category | flops | bytes accessed | tf_op | source)
XLA Modules:
  0.0 1483.9 jit_solution(4408652994084007588)
XLA Ops:
  16.1 33.4 %all-gather.1 = bf16[1,1024,256]{2,1,0:T(8,128)(2,1)S(1)} all-gather(bf16[1,128,256]{2,1,0:T(8,128)(2,1)S(1)} %get-tuple-element.102), channel_id=3, replica_groups=mesh['dp'=8,'mp'=4] {'dp'}, dimensions={1}, use_global_device_ids=true | all-gather | bytes 589824 | tf_op jit(solution)/shard_map/all_gather | solution.py:291
  49.7 30.1 %all-gather.39.cloned.1.call-done = bf16[1,1024,768]{2,1,0:T(8,128)(2,1)} async-done(((bf16[1,128,768]{2,1,0:T(8,128)(2,1)}), bf16[1,1024,768]{2,1,0:T(8,128)(2,1)}) %all-gather.39.cloned.1.call-update) | async-done | bytes 1572880 | tf_op jit(solution)/shard_map/all_gather | solution.py:290
  89.9 28.6 %reduce-scatter.17.cloned.1.call-done = f32[128,1024]{1,0:T(8,128)} async-done(((f32[512,1024]{1,0:T(8,128)}), f32[128,1024]{1,0:T(8,128)}) %reduce-scatter.17.cloned.1.call-update) | async-done | bytes 524304 | tf_op jit(solution)/shard_map/reduce_scatter | solution.py:118
  122.7 47.4 %all-gather.41.cloned.1.call-done = bf16[1,1024,1024]{2,1,0:T(8,128)(2,1)} async-done(((bf16[1,128,1024]{2,1,0:T(8,128)(2,1)}), bf16[1,1024,1024]{2,1,0:T(8,128)(2,1)}) %all-gather.41.cloned.1.call-update) | async-done | bytes 2097168 | tf_op jit(solution)/shard_map/all_gather | solution.py:292
  170.2 17.2 %all-gather.25.cloned.1.call-done = bf16[512,1024]{1,0:T(8,128)(2,1)} async-done(((bf16[128,1024]{1,0:T(8,128)(2,1)}), bf16[512,1024]{1,0:T(8,128)(2,1)}) %all-gather.25.cloned.1.call-update) | async-done | bytes 1048592 | tf_op jit(solution)/shard_map/all_gather | solution.py:106
  190.6 48.5 %all-gather.43.cloned.1.call-done = bf16[1,1024,1024]{2,1,0:T(8,128)(2,1)} async-done(((bf16[1,128,1024]{2,1,0:T(8,128)(2,1)}), bf16[1,1024,1024]{2,1,0:T(8,128)(2,1)}) %all-gather.43.cloned.1.call-update) | async-done | bytes 2097168 | tf_op jit(solution)/shard_map/all_gather | solution.py:293
  244.3 29.0 %reduce-scatter.19.cloned.1.call-done = f32[128,1024]{1,0:T(8,128)} async-done(((f32[512,1024]{1,0:T(8,128)}), f32[128,1024]{1,0:T(8,128)}) %reduce-scatter.19.cloned.1.call-update) | async-done | bytes 524304 | tf_op jit(solution)/shard_map/reduce_scatter | solution.py:118
  275.7 32.4 %all-gather.5 = bf16[1,1024,256]{2,1,0:T(8,128)(2,1)S(1)} all-gather(bf16[1,128,256]{2,1,0:T(8,128)(2,1)S(1)} %get-tuple-element.101), channel_id=7, replica_groups=mesh['dp'=8,'mp'=4] {'dp'}, dimensions={1}, use_global_device_ids=true | all-gather | bytes 589824 | tf_op jit(solution)/shard_map/all_gather | solution.py:291
  308.1 12.9 all-gather.45.cloned.1.call-done
  321.0 18.0 %all-gather.27.cloned.1.call-done = bf16[512,1024]{1,0:T(8,128)(2,1)} async-done(((bf16[128,1024]{1,0:T(8,128)(2,1)}), bf16[512,1024]{1,0:T(8,128)(2,1)}) %all-gather.27.cloned.1.call-update) | async-done | bytes 1048592 | tf_op jit(solution)/shard_map/all_gather | solution.py:106
  352.3 30.5 %reduce-scatter.21.cloned.1.call-done = f32[128,1024]{1,0:T(8,128)} async-done(((f32[512,1024]{1,0:T(8,128)}), f32[128,1024]{1,0:T(8,128)}) %reduce-scatter.21.cloned.1.call-update) | async-done | bytes 524304 | tf_op jit(solution)/shard_map/reduce_scatter | solution.py:118
  386.6 48.1 %all-gather.47.cloned.1.call-done = bf16[1,1024,1024]{2,1,0:T(8,128)(2,1)} async-done(((bf16[1,128,1024]{2,1,0:T(8,128)(2,1)}), bf16[1,1024,1024]{2,1,0:T(8,128)(2,1)}) %all-gather.47.cloned.1.call-update) | async-done | bytes 2097168 | tf_op jit(solution)/shard_map/all_gather | solution.py:292
  434.7 17.3 %all-gather.29.cloned.1.call-done = bf16[512,1024]{1,0:T(8,128)(2,1)} async-done(((bf16[128,1024]{1,0:T(8,128)(2,1)}), bf16[512,1024]{1,0:T(8,128)(2,1)}) %all-gather.29.cloned.1.call-update) | async-done | bytes 1048592 | tf_op jit(solution)/shard_map/all_gather | solution.py:106
  456.4 14.4 all-gather.31.cloned.1.call-done
  470.8 51.7 %all-gather.49.cloned.1.call-done = bf16[1,1024,1024]{2,1,0:T(8,128)(2,1)} async-done(((bf16[1,128,1024]{2,1,0:T(8,128)(2,1)}), bf16[1,1024,1024]{2,1,0:T(8,128)(2,1)}) %all-gather.49.cloned.1.call-update) | async-done | bytes 2097168 | tf_op jit(solution)/shard_map/all_gather | solution.py:293
  536.2 24.7 %reduce-scatter.25.cloned.1.call-done = f32[128,1024]{1,0:T(8,128)} async-done(((f32[512,1024]{1,0:T(8,128)}), f32[128,1024]{1,0:T(8,128)}) %reduce-scatter.25.cloned.1.call-update) | async-done | bytes 524304 | tf_op jit(solution)/shard_map/reduce_scatter | solution.py:131
  562.8 31.7 %reduce-scatter.23.cloned.1.call-done = f32[128,1024]{1,0:T(8,128)} async-done(((f32[512,1024]{1,0:T(8,128)}), f32[128,1024]{1,0:T(8,128)}) %reduce-scatter.23.cloned.1.call-update) | async-done | bytes 524304 | tf_op jit(solution)/shard_map/reduce_scatter | solution.py:118
  597.9 16.6 %all-gather.33.cloned.1.call-done = bf16[512,1024]{1,0:T(8,128)(2,1)} async-done(((bf16[128,1024]{1,0:T(8,128)(2,1)}), bf16[512,1024]{1,0:T(8,128)(2,1)}) %all-gather.33.cloned.1.call-update) | async-done | bytes 1048592 | tf_op jit(solution)/shard_map/all_gather | solution.py:110
  627.7 31.3 %reduce-scatter.27.cloned.1.call-done = f32[128,1024]{1,0:T(8,128)} async-done(((f32[512,1024]{1,0:T(8,128)}), f32[128,1024]{1,0:T(8,128)}) %reduce-scatter.27.cloned.1.call-update) | async-done | bytes 524304 | tf_op jit(solution)/shard_map/reduce_scatter | solution.py:131
  663.6 16.8 %all-gather.35.cloned.1.call-done = bf16[512,1024]{1,0:T(8,128)(2,1)} async-done(((bf16[128,1024]{1,0:T(8,128)(2,1)}), bf16[512,1024]{1,0:T(8,128)(2,1)}) %all-gather.35.cloned.1.call-update) | async-done | bytes 1048592 | tf_op jit(solution)/shard_map/all_gather | solution.py:110
  680.4 5.6 fusion.136
  688.7 31.3 %reduce-scatter.29.cloned.1.call-done = f32[128,1024]{1,0:T(8,128)} async-done(((f32[512,1024]{1,0:T(8,128)}), f32[128,1024]{1,0:T(8,128)}) %reduce-scatter.29.cloned.1.call-update) | async-done | bytes 524304 | tf_op jit(solution)/shard_map/reduce_scatter | solution.py:131
  765.4 48.0 %reduce-scatter.47.cloned.1.call-done = bf16[128,1024]{1,0:T(8,128)(2,1)} async-done(((bf16[1024,1024]{1,0:T(8,128)(2,1)}), bf16[128,1024]{1,0:T(8,128)(2,1)}) %reduce-scatter.47.cloned.1.call-update) | async-done | bytes 262160 | tf_op jit(solution)/shard_map/reduce_scatter | solution.py:322
  815.5 69.4 %reduce-scatter.43.cloned.1.call-done = bf16[128,1024]{1,0:T(8,128)(2,1)} async-done(((bf16[1024,1024]{1,0:T(8,128)(2,1)}), bf16[128,1024]{1,0:T(8,128)(2,1)}) %reduce-scatter.43.cloned.1.call-update) | async-done | bytes 262160 | tf_op jit(solution)/shard_map/reduce_scatter | solution.py:319
  887.2 63.2 %reduce-scatter.39.cloned.1.call-done = bf16[128,256]{1,0:T(8,128)(2,1)} async-done(((bf16[1024,256]{1,0:T(8,128)(2,1)}), bf16[128,256]{1,0:T(8,128)(2,1)}) %reduce-scatter.39.cloned.1.call-update) | async-done | bytes 65552 | tf_op jit(solution)/shard_map/reduce_scatter | solution.py:316
  952.0 67.2 %reduce-scatter.35.cloned.1.call-done = bf16[128,768]{1,0:T(8,128)(2,1)} async-done(((bf16[1024,768]{1,0:T(8,128)(2,1)}), bf16[128,768]{1,0:T(8,128)(2,1)}) %reduce-scatter.35.cloned.1.call-update) | async-done | bytes 196624 | tf_op jit(solution)/shard_map/reduce_scatter | solution.py:313
  1023.4 66.4 %reduce-scatter.45.cloned.1.call-done = bf16[128,1024]{1,0:T(8,128)(2,1)} async-done(((bf16[1024,1024]{1,0:T(8,128)(2,1)}), bf16[128,1024]{1,0:T(8,128)(2,1)}) %reduce-scatter.45.cloned.1.call-update) | async-done | bytes 262160 | tf_op jit(solution)/shard_map/reduce_scatter | solution.py:322
  1100.2 61.0 %reduce-scatter.41.cloned.1.call-done = bf16[128,1024]{1,0:T(8,128)(2,1)} async-done(((bf16[1024,1024]{1,0:T(8,128)(2,1)}), bf16[128,1024]{1,0:T(8,128)(2,1)}) %reduce-scatter.41.cloned.1.call-update) | async-done | bytes 262160 | tf_op jit(solution)/shard_map/reduce_scatter | solution.py:319
  1172.4 54.0 %reduce-scatter.37.cloned.1.call-done = bf16[128,256]{1,0:T(8,128)(2,1)} async-done(((bf16[1024,256]{1,0:T(8,128)(2,1)}), bf16[128,256]{1,0:T(8,128)(2,1)}) %reduce-scatter.37.cloned.1.call-update) | async-done | bytes 65552 | tf_op jit(solution)/shard_map/reduce_scatter | solution.py:316
  1231.0 63.4 %reduce-scatter.33.cloned.1.call-done = bf16[128,768]{1,0:T(8,128)(2,1)} async-done(((bf16[1024,768]{1,0:T(8,128)(2,1)}), bf16[128,768]{1,0:T(8,128)(2,1)}) %reduce-scatter.33.cloned.1.call-update) | async-done | bytes 196624 | tf_op jit(solution)/shard_map/reduce_scatter | solution.py:313
  1299.7 27.1 %reduce-scatter.31.cloned.1.call-done = f32[128,1024]{1,0:T(8,128)} async-done(((f32[512,1024]{1,0:T(8,128)}), f32[128,1024]{1,0:T(8,128)}) %reduce-scatter.31.cloned.1.call-update) | async-done | bytes 524304 | tf_op jit(solution)/shard_map/reduce_scatter | solution.py:131
  1331.5 128.1 %all-reduce.3.cloned.1.call-done = (f32[2,2,1024]{2,1,0:T(2,128)}, f32[2,2,1024]{2,1,0:T(2,128)}, f32[2,3072]{1,0:T(2,128)}, f32[2,2,1024]{2,1,0:T(2,128)}, f32[2,4096]{1,0:T(2,128)}) async-done(((f32[2,2,1024]{2,1,0:T(2,128)}, f32[2,2,1024]{2,1,0:T(2,128)}, f32[2,3072]{1,0:T(2,128)}, f32[2,2,1024]{2,1,0:T(2,128)}, f32[2,4096]{1,0:T(2,128)}), (f32[2,2,1024]{2,1,0:T(2,128)}, f32[2,2,1024]{2,1,0:T(2,128)}, ...) | async-done | bytes 106512 | tf_op jit(solution)/shard_map/psum | solution.py:346
  (407 shorter events, 202.6 us)
Async XLA Ops:
  7.2 42.5 %all-gather.23.cloned.1.call-start = ((), (), s32[]{:S(2)}) async-start(), calls=%async_computation.16 | async-start | bytes 1310720 | tf_op jit(solution)/shard_map/all_gather | solution.py:106
  13.3 66.5 %all-gather.39.cloned.1.call-start = ((), (), s32[]{:S(2)}) async-start(), calls=%async_computation.40 | async-start | bytes 1769472 | tf_op jit(solution)/shard_map/all_gather | solution.py:290
  14.2 104.3 %reduce-scatter.17.cloned.1.call-start = ((), (), s32[]{:S(2)}) async-start(), calls=%async_computation.17 | async-start | bytes 2621440 | tf_op jit(solution)/shard_map/reduce_scatter | solution.py:118
  88.8 81.3 %all-gather.41.cloned.1.call-start = ((), (), s32[]{:S(2)}) async-start(), calls=%async_computation.41 | async-start | bytes 2359296 | tf_op jit(solution)/shard_map/all_gather | solution.py:292
  89.8 97.6 %all-gather.25.cloned.1.call-start = ((), (), s32[]{:S(2)}) async-start(), calls=%async_computation.18 | async-start | bytes 1310720 | tf_op jit(solution)/shard_map/all_gather | solution.py:106
  120.8 118.3 %all-gather.43.cloned.1.call-start = ((), (), s32[]{:S(2)}) async-start(), calls=%async_computation.42 | async-start | bytes 2359296 | tf_op jit(solution)/shard_map/all_gather | solution.py:293
  121.8 151.5 %reduce-scatter.19.cloned.1.call-start = ((), (), s32[]{:S(2)}) async-start(), calls=%async_computation.19 | async-start | bytes 2621440 | tf_op jit(solution)/shard_map/reduce_scatter | solution.py:118
  243.5 77.5 %all-gather.45.cloned.1.call-start = ((), (), s32[]{:S(2)}) async-start(), calls=%async_computation.43 | async-start | bytes 1769472 | tf_op jit(solution)/shard_map/all_gather | solution.py:290
  244.3 94.7 %all-gather.27.cloned.1.call-start = ((), (), s32[]{:S(2)}) async-start(), calls=%async_computation.20 | async-start | bytes 1310720 | tf_op jit(solution)/shard_map/all_gather | solution.py:106
  275.7 107.2 %reduce-scatter.21.cloned.1.call-start = ((), (), s32[]{:S(2)}) async-start(), calls=%async_computation.21 | async-start | bytes 2621440 | tf_op jit(solution)/shard_map/reduce_scatter | solution.py:118
  351.6 83.1 %all-gather.47.cloned.1.call-start = ((), (), s32[]{:S(2)}) async-start(), calls=%async_computation.44 | async-start | bytes 2359296 | tf_op jit(solution)/shard_map/all_gather | solution.py:292
  352.3 99.6 %all-gather.29.cloned.1.call-start = ((), (), s32[]{:S(2)}) async-start(), calls=%async_computation.22 | async-start | bytes 1310720 | tf_op jit(solution)/shard_map/all_gather | solution.py:106
  385.2 85.6 %all-gather.31.cloned.1.call-start = ((), (), s32[]{:S(2)}) async-start(), calls=%async_computation.24 | async-start | bytes 1310720 | tf_op jit(solution)/shard_map/all_gather | solution.py:110
  386.0 136.5 %all-gather.49.cloned.1.call-start = ((), (), s32[]{:S(2)}) async-start(), calls=%async_computation.45 | async-start | bytes 2359296 | tf_op jit(solution)/shard_map/all_gather | solution.py:293
  386.6 174.4 %reduce-scatter.25.cloned.1.call-start = ((), (), s32[]{:S(2)}) async-start(), calls=%async_computation.25 | async-start | bytes 2621440 | tf_op jit(solution)/shard_map/reduce_scatter | solution.py:131
  531.1 63.4 %reduce-scatter.23.cloned.1.call-start = ((), (), s32[]{:S(2)}) async-start(), calls=%async_computation.23 | async-start | bytes 2621440 | tf_op jit(solution)/shard_map/reduce_scatter | solution.py:118
  536.2 78.3 %all-gather.33.cloned.1.call-start = ((), (), s32[]{:S(2)}) async-start(), calls=%async_computation.26 | async-start | bytes 1310720 | tf_op jit(solution)/shard_map/all_gather | solution.py:110
  597.7 61.3 %reduce-scatter.27.cloned.1.call-start = ((), (), s32[]{:S(2)}) async-start(), calls=%async_computation.27 | async-start | bytes 2621440 | tf_op jit(solution)/shard_map/reduce_scatter | solution.py:131
  627.7 52.7 %all-gather.35.cloned.1.call-start = ((), (), s32[]{:S(2)}) async-start(), calls=%async_computation.28 | async-start | bytes 1310720 | tf_op jit(solution)/shard_map/all_gather | solution.py:110
  663.6 56.4 %reduce-scatter.29.cloned.1.call-start = ((), (), s32[]{:S(2)}) async-start(), calls=%async_computation.29 | async-start | bytes 2621440 | tf_op jit(solution)/shard_map/reduce_scatter | solution.py:131
  688.7 59.9 %all-gather.37.cloned.1.call-start = ((), (), s32[]{:S(2)}) async-start(), calls=%async_computation.30 | async-start | bytes 1310720 | tf_op jit(solution)/shard_map/all_gather | solution.py:110
  724.5 88.9 %reduce-scatter.47.cloned.1.call-start = ((), (), s32[]{:S(2)}) async-start(), calls=%async_computation.39 | async-start | bytes 2359296 | tf_op jit(solution)/shard_map/reduce_scatter | solution.py:322
  729.3 155.6 %reduce-scatter.43.cloned.1.call-start = ((), (), s32[]{:S(2)}) async-start(), calls=%async_computation.37 | async-start | bytes 2359296 | tf_op jit(solution)/shard_map/reduce_scatter | solution.py:319
  733.4 217.0 %reduce-scatter.39.cloned.1.call-start = ((), (), s32[]{:S(2)}) async-start(), calls=%async_computation.35 | async-start | bytes 589824 | tf_op jit(solution)/shard_map/reduce_scatter | solution.py:316
  736.0 283.1 %reduce-scatter.35.cloned.1.call-start = ((), (), s32[]{:S(2)}) async-start(), calls=%async_computation.33 | async-start | bytes 1769472 | tf_op jit(solution)/shard_map/reduce_scatter | solution.py:313
  739.8 350.0 %reduce-scatter.45.cloned.1.call-start = ((), (), s32[]{:S(2)}) async-start(), calls=%async_computation.38 | async-start | bytes 2359296 | tf_op jit(solution)/shard_map/reduce_scatter | solution.py:322
  744.3 417.0 %reduce-scatter.41.cloned.1.call-start = ((), (), s32[]{:S(2)}) async-start(), calls=%async_computation.36 | async-start | bytes 2359296 | tf_op jit(solution)/shard_map/reduce_scatter | solution.py:319
  748.4 478.0 %reduce-scatter.37.cloned.1.call-start = ((), (), s32[]{:S(2)}) async-start(), calls=%async_computation.34 | async-start | bytes 589824 | tf_op jit(solution)/shard_map/reduce_scatter | solution.py:316
  757.0 537.4 %reduce-scatter.33.cloned.1.call-start = ((), (), s32[]{:S(2)}) async-start(), calls=%async_computation.32 | async-start | bytes 1769472 | tf_op jit(solution)/shard_map/reduce_scatter | solution.py:313
  765.3 561.4 %reduce-scatter.31.cloned.1.call-start = ((), (), s32[]{:S(2)}) async-start(), calls=%async_computation.31 | async-start | bytes 2621440 | tf_op jit(solution)/shard_map/reduce_scatter | solution.py:131
  815.5 207.3 %copy-start.66 = (f32[1024]{0:T(1024)S(1)}, f32[1024]{0:T(1024)}, u32[]{:S(2)}) copy-start(f32[1024]{0:T(1024)} %get-tuple-element.62) | copy-start | bytes 12292
  1095.6 364.0 %all-reduce.3.cloned.1.call-start = ((), (), s32[]{:S(2)}) async-start(), calls=%async_computation.46 | async-start | bytes 212992 | tf_op jit(solution)/shard_map/psum | solution.py:346
  (90 other events, 4374.7 us)
Sparse Core Ops, SparseCore 0:
  13.4 19.4 all-gather.22
  35.7 44.0 all-gather.38
  88.9 29.5 reduce-scatter.16
  121.1 49.0 all-gather.40
  172.1 15.2 all-gather.24
  190.0 49.0 all-gather.42
  243.6 29.6 reduce-scatter.18
  276.1 44.8 all-gather.44
  323.1 15.8 all-gather.26
  351.7 31.1 reduce-scatter.20
  385.6 49.0 all-gather.46
  436.7 15.2 all-gather.28
  454.1 16.6 all-gather.30
  473.3 49.0 all-gather.48
  531.2 29.6 reduce-scatter.24
  563.3 31.1 reduce-scatter.22
  597.8 16.6 all-gather.32
  627.8 31.1 reduce-scatter.26
  663.7 16.6 all-gather.34
  688.8 31.1 reduce-scatter.28
  724.6 16.6 all-gather.36
  744.9 68.4 reduce-scatter.46
  817.5 67.3 reduce-scatter.42
  888.6 61.7 reduce-scatter.38
  954.4 64.6 reduce-scatter.34
  1022.5 67.1 reduce-scatter.44
  1093.7 67.4 reduce-scatter.40
  1164.6 61.7 reduce-scatter.36
  1229.8 64.4 reduce-scatter.32
  1296.7 29.9 reduce-scatter.30
  1334.9 124.6 all-reduce.2
where the time goes:
time: 1490 us; the launch traced here: 1480 us
  waiting for transfers between devices  1200 us (81%)
  matrix products  95 us (6%)
  other arithmetic  77.1 us (5%)
  blocking collectives  65.8 us (4%)
  local copies, waits for them, and re-layouts  31.9 us (2%)
  between operations  16.1 us (1%)
    reduce_scatter x2, waiting for transfers between devices, per_device(): lax.psum_scatter(weight_grads[0].astype(jnp.bfloat16), 'dp', scatter_dime...  131 us
    reduce_scatter x2, waiting for transfers between devices, per_device(): lax.psum_scatter(weight_grads[2].astype(jnp.bfloat16), 'dp', scatter_dime...  130 us
    psum x1, waiting for transfers between devices, per_device(): lax.psum((gain_part, nbias_part, qbias_part, obias_part, ubias_part), ('d...  128 us
    reduce_scatter x4, waiting for transfers between devices, project_sum(): lax.psum_scatter(term(jnp.int32(0), left.shape[0] // lax.axis_size('mp')...  120 us
    reduce_scatter x2, waiting for transfers between devices, per_device(): lax.psum_scatter(weight_grads[1].astype(jnp.bfloat16), 'dp', scatter_dime...  117 us
    reduce_scatter x4, waiting for transfers between devices, project_back(): lax.psum_scatter(term(jnp.int32(0), left.shape[0] // lax.axis_size('mp')...  114 us
    reduce_scatter x2, waiting for transfers between devices, per_device(): lax.psum_scatter(weight_grads[3].astype(jnp.bfloat16), 'dp', scatter_dime...  114 us
    all_gather x2, waiting for transfers between devices, per_device(): lax.all_gather(w_down[layer_idx].astype(jnp.bfloat16), 'dp', axis=0, tile...  100 us
  transfers between devices with their start and end apart: 31, of which 29 were waited for; matrix products, arithmetic and copies ran while one was open for 7% of the time, Pallas kernels for 0%

commit v1 on v0

--- a/solution.py
+++ b/solution.py
@@ -1,6 +1,10 @@
+import functools
+
 import jax
 import jax.numpy as jnp
 from jax import lax
+from jax.experimental import pallas as pl
+from jax.experimental.pallas import tpu as pltpu
 from jax.sharding import PartitionSpec as P
 
 HEADS = 16
@@ -102,38 +106,124 @@
     return jnp.stack([grad_queries, grad_keys, grad_values], axis=2).reshape(row_count, -1)
 
 
+def greet_peers(own, count):
+    barrier = pltpu.get_barrier_semaphore()
+    for step in range(1, count):
+        pl.semaphore_signal(
+            barrier,
+            inc=1,
+            device_id={"mp": lax.rem(own + step, count)},
+            device_id_type=pl.DeviceIdType.MESH,
+        )
+    pl.semaphore_wait(barrier, count - 1)
+
+
+def gather_kernel(count, rows_ref, out_ref, send_sems, recv_sems):
+    own = lax.axis_index("mp")
+    rows = rows_ref.shape[0]
+    greet_peers(own, count)
+
+    def block_of(index):
+        return out_ref.at[pl.ds(pl.multiple_of(index * rows, rows), rows)]
+
+    copies = []
+    for step in range(1, count):
+        copy = pltpu.make_async_remote_copy(
+            src_ref=rows_ref,
+            dst_ref=block_of(own),
+            send_sem=send_sems.at[step - 1],
+            recv_sem=recv_sems.at[step - 1],
+            device_id={"mp": lax.rem(own + step, count)},
+            device_id_type=pl.DeviceIdType.MESH,
+        )
+        copy.start()
+        copies.append(copy)
+    out_ref[pl.ds(pl.multiple_of(own * rows, rows), rows), :] = rows_ref[...]
+    for copy in copies:
+        copy.wait()
+
+
+def scatter_kernel(count, parts_ref, out_ref, landed, send_sems, recv_sems):
+    own = lax.axis_index("mp")
+    rows = out_ref.shape[0]
+    greet_peers(own, count)
+    copies = []
+    for step in range(1, count):
+        dest = lax.rem(own + step, count)
+        copy = pltpu.make_async_remote_copy(
+            src_ref=parts_ref.at[pl.ds(pl.multiple_of(dest * rows, rows), rows)],
+            dst_ref=landed.at[step - 1],
+            send_sem=send_sems.at[step - 1],
+            recv_sem=recv_sems.at[step - 1],
+            device_id={"mp": dest},
+            device_id_type=pl.DeviceIdType.MESH,
+        )
+        copy.start()
+        copies.append(copy)
+    for copy in copies:
+        copy.wait()
+    total = parts_ref[pl.ds(pl.multiple_of(own * rows, rows), rows), :].astype(jnp.float32)
+    for step in range(1, count):
+        total = total + landed[step - 1].astype(jnp.float32)
+    out_ref[...] = total
+
+
+transfer_cost = pl.CostEstimate(flops=0, bytes_accessed=40_000_000, transcendentals=0)
+
+
+def gather_rows(own_rows):
+    count = lax.axis_size("mp")
+    rows, cols = own_rows.shape
+    return pl.pallas_call(
+        functools.partial(gather_kernel, count),
+        out_shape=jax.ShapeDtypeStruct((rows * count, cols), own_rows.dtype),
+        in_specs=[pl.BlockSpec(memory_space=pltpu.VMEM)],
+        out_specs=pl.BlockSpec(memory_space=pltpu.VMEM),
+        scratch_shapes=[
+            pltpu.SemaphoreType.DMA((count - 1,)),
+            pltpu.SemaphoreType.DMA((count - 1,)),
+        ],
+        compiler_params=pltpu.CompilerParams(collective_id=1, has_side_effects=True),
+        cost_estimate=transfer_cost,
+        name="gather_rows",
+    )(own_rows)
+
+
+def scatter_rows(parts):
+    count = lax.axis_size("mp")
+    rows, cols = parts.shape[0] // count, parts.shape[1]
+    return pl.pallas_call(
+        functools.partial(scatter_kernel, count),
+        out_shape=jax.ShapeDtypeStruct((rows, cols), jnp.float32),
+        in_specs=[pl.BlockSpec(memory_space=pltpu.VMEM)],
+        out_specs=pl.BlockSpec(memory_space=pltpu.VMEM),
+        scratch_shapes=[
+            pltpu.VMEM((count - 1, rows, cols), parts.dtype),
+            pltpu.SemaphoreType.DMA((count - 1,)),
+            pltpu.SemaphoreType.DMA((count - 1,)),
+        ],
+        compiler_params=pltpu.CompilerParams(collective_id=2, has_side_effects=True),
+        cost_estimate=transfer_cost,
+        name="scatter_rows",
+    )(parts)
+
+
 def gather_norm(normed_rows):
-    return lax.all_gather(normed_rows, "mp", axis=0, tiled=True)
+    return gather_rows(normed_rows)
 
 
 def gather_cot(grad_rows):
-    return lax.all_gather(grad_rows, "mp", axis=0, tiled=True)
+    return gather_rows(grad_rows)
 
 
 def project_sum(left, right):
-
-    def term(row_start, row_count):
-        return lax.dot_general(left, right, contract_cols, preferred_element_type=jnp.float32)
-
-    return lax.psum_scatter(
-        term(jnp.int32(0), left.shape[0] // lax.axis_size("mp") * lax.axis_size("mp")),
-        "mp",
-        scatter_dimension=0,
-        tiled=True,
-    )
+    parts = lax.dot_general(left, right, contract_cols, preferred_element_type=jnp.float32)
+    return scatter_rows(parts.astype(jnp.bfloat16))
 
 
 def project_back(left, right):
-
-    def term(row_start, row_count):
-        return lax.dot_general(left, right, contract_cols, preferred_element_type=jnp.float32)
-
-    return lax.psum_scatter(
-        term(jnp.int32(0), left.shape[0] // lax.axis_size("mp") * lax.axis_size("mp")),
-        "mp",
-        scatter_dimension=0,
-        tiled=True,
-    )
+    parts = lax.dot_general(left, right, contract_cols, preferred_element_type=jnp.float32)
+    return scatter_rows(parts.astype(jnp.bfloat16))
 
 
 def local_parts(weight_pairs):
@@ -179,7 +269,7 @@
     )
 
 
-def backward_layer(upstream, seg_row, matrices, vectors, saved, slopes):
+def backward_layer(upstream, seg_row, matrices, vectors, saved, slopes, early=None):
     w_joined, w_proj, w_expand, w_shrink = matrices
     gain_vec, shift_vec, joined_bias, out_shift, expand_bias = vectors
     (
@@ -203,6 +293,10 @@
     gain_two = jnp.sum(grad_norm_two * normed_two, axis=0)
     shift_two = jnp.sum(grad_norm_two, axis=0)
     middle = upstream + norm_backward(grad_norm_two, normed_two, inv_two, gain_vec[1])
+    early_sums = None
+    if early is not None:
+        early_parts = local_parts(((rows_two, pre_rounded), (grad_rows, hidden_act)))
+        middle, early_sums = early(middle, early_parts)
     grad_rows_one = gather_cot(middle.astype(jnp.bfloat16))
     grad_mixed = jnp.dot(grad_rows_one, w_proj, preferred_element_type=jnp.float32).astype(
         jnp.bfloat16
@@ -216,9 +310,12 @@
     weight_pairs = (
         (rows_one, joined_rounded),
         (grad_rows_one, mixed),
-        (rows_two, pre_rounded),
-        (grad_rows, hidden_act),
-    )
+    )
+    if early is None:
+        weight_pairs = weight_pairs + (
+            (rows_two, pre_rounded),
+            (grad_rows, hidden_act),
+        )
     small_grads = (
         jnp.stack([gain_one, gain_two]),
         jnp.stack([shift_one, shift_two]),
@@ -226,7 +323,7 @@
         jnp.stack([jnp.sum(middle, axis=0), jnp.sum(upstream, axis=0)]),
         jnp.sum(grad_pre, axis=0),
     )
-    return (grad_below, weight_pairs, small_grads)
+    return (grad_below, weight_pairs, small_grads, early_sums)
 
 
 def adamw(weight, gradient, moments, decay):
@@ -282,70 +379,121 @@
             up_local[layer_idx],
         )
 
+    layer_ids = range(layer_count)
+    shards = [
+        tuple(w[layer_idx].astype(jnp.bfloat16) for w in (w_qkv, w_dense, w_up, w_down))
+        for layer_idx in layer_ids
+    ]
+
+    def gather_joined(pieces):
+        whole = lax.all_gather(jnp.concatenate(pieces, axis=1), "dp", axis=0, tiled=True)
+        return split_cols(whole, [piece.shape[1] for piece in pieces])
+
+    def split_cols(whole, widths):
+        taken, start = [], 0
+        for width in widths:
+            taken.append(lax.slice_in_dim(whole, start, start + width, axis=1))
+            start += width
+        return tuple(taken)
+
+    matrices_of = []
+    for layer_idx in layer_ids:
+        if layer_idx == 0:
+            matrices_of.append(
+                gather_joined(shards[0][:2]) + gather_joined(shards[0][2:])
+            )
+        else:
+            matrices_of.append(gather_joined(shards[layer_idx]))
     stream = hidden_in
-    kept_mats = []
     kept_acts = []
-    for layer_idx in range(layer_count):
-        matrices = (
-            lax.all_gather(w_qkv[layer_idx].astype(jnp.bfloat16), "dp", axis=0, tiled=True),
-            lax.all_gather(w_dense[layer_idx].astype(jnp.bfloat16), "dp", axis=0, tiled=True),
-            lax.all_gather(w_up[layer_idx].astype(jnp.bfloat16), "dp", axis=0, tiled=True),
-            lax.all_gather(w_down[layer_idx].astype(jnp.bfloat16), "dp", axis=0, tiled=True),
-        )
-        stream, saved = forward_layer(stream, seg_row, matrices, vectors_of(layer_idx), slopes)
-        kept_mats.append(matrices)
+    for layer_idx in layer_ids:
+        stream, saved = forward_layer(
+            stream, seg_row, matrices_of[layer_idx], vectors_of(layer_idx), slopes
+        )
         kept_acts.append(saved)
     upstream = cotangent
     reduced = [None] * layer_count
     small_parts = [None] * layer_count
-    for layer_idx in reversed(range(layer_count)):
-        matrices = (
-            lax.all_gather(w_qkv[layer_idx].astype(jnp.bfloat16), "dp", axis=0, tiled=True),
-            lax.all_gather(w_dense[layer_idx].astype(jnp.bfloat16), "dp", axis=0, tiled=True),
-            lax.all_gather(w_up[layer_idx].astype(jnp.bfloat16), "dp", axis=0, tiled=True),
-            lax.all_gather(w_down[layer_idx].astype(jnp.bfloat16), "dp", axis=0, tiled=True),
-        )
-        upstream, weight_pairs, small_grads = backward_layer(
-            upstream, seg_row, matrices, vectors_of(layer_idx), kept_acts[layer_idx], slopes
-        )
-        weight_grads = local_parts(weight_pairs)
-        reduced[layer_idx] = (
-            lax.psum_scatter(
-                weight_grads[0].astype(jnp.bfloat16), "dp", scatter_dimension=0, tiled=True
-            ).astype(jnp.float32),
-            lax.psum_scatter(
-                weight_grads[1].astype(jnp.bfloat16), "dp", scatter_dimension=0, tiled=True
-            ).astype(jnp.float32),
-            lax.psum_scatter(
-                weight_grads[2].astype(jnp.bfloat16), "dp", scatter_dimension=0, tiled=True
-            ).astype(jnp.float32),
-            lax.psum_scatter(
-                weight_grads[3].astype(jnp.bfloat16), "dp", scatter_dimension=0, tiled=True
-            ).astype(jnp.float32),
+    dp_count = lax.axis_size("dp")
+    own_rows = w_qkv.shape[1]
+    lanes = 128
+
+    def join_parts(pieces):
+        return jnp.concatenate([piece.astype(jnp.bfloat16) for piece in pieces], axis=1)
+
+    def scatter_joined(joined):
+        return lax.psum_scatter(joined, "dp", scatter_dimension=0, tiled=True)
+
+    def start_early(middle, early_parts):
+        middle, joined = lax.optimization_barrier((middle, join_parts(early_parts)))
+        if layer_count > 1:
+            joined, reduced[1] = lax.optimization_barrier((joined, reduced[1]))
+        return (middle, scatter_joined(joined))
+
+    widths = [qkv_cols, w_dense.shape[2], up_cols, w_down.shape[2]]
+    for layer_idx in reversed(layer_ids):
+        upstream, weight_pairs, small_grads, early_sum = backward_layer(
+            upstream,
+            seg_row,
+            matrices_of[layer_idx],
+            vectors_of(layer_idx),
+            kept_acts[layer_idx],
+            slopes,
+            start_early if layer_idx == 0 else None,
         )
         small_parts[layer_idx] = small_grads
-    qkv_grad = jnp.stack([reduced[layer_idx][0] for layer_idx in range(layer_count)])
-    dense_grad = jnp.stack([reduced[layer_idx][1] for layer_idx in range(layer_count)])
-    up_grad = jnp.stack([reduced[layer_idx][2] for layer_idx in range(layer_count)])
-    down_grad = jnp.stack([reduced[layer_idx][3] for layer_idx in range(layer_count)])
-
-    def widen(small_piece, total_len):
-        return lax.dynamic_update_slice_in_dim(
-            jnp.zeros((total_len,), jnp.float32), small_piece, mp_index * small_piece.shape[0], 0
-        )
-
-    gain_part = jnp.stack([small_parts[layer_idx][0] for layer_idx in range(layer_count)])
-    nbias_part = jnp.stack([small_parts[layer_idx][1] for layer_idx in range(layer_count)])
-    qbias_part = jnp.stack(
-        [widen(small_parts[layer_idx][2], qkv_bias.shape[1]) for layer_idx in range(layer_count)]
-    )
-    obias_part = jnp.stack([small_parts[layer_idx][3] for layer_idx in range(layer_count)])
-    ubias_part = jnp.stack(
-        [widen(small_parts[layer_idx][4], up_bias.shape[1]) for layer_idx in range(layer_count)]
-    )
-    gain_grad, nbias_grad, qbias_grad, obias_grad, ubias_grad = lax.psum(
-        (gain_part, nbias_part, qbias_part, obias_part, ubias_part), ("dp", "mp")
-    )
+        parts = local_parts(weight_pairs)
+        if layer_idx > 0:
+            upstream, joined = lax.optimization_barrier((upstream, join_parts(parts)))
+            reduced[layer_idx] = scatter_joined(joined)
+            continue
+        shared_part = jnp.concatenate(
+            [jnp.stack([part[i] for part in small_parts]).reshape(-1) for i in (0, 1, 3)]
+        )
+        local_part = jnp.concatenate(
+            [jnp.stack([part[i] for part in small_parts]).reshape(-1) for i in (2, 4)]
+        )
+        small_vec = jnp.concatenate([shared_part, local_part])
+        small_len = small_vec.shape[0]
+        small_rows = -(-small_len // (dp_count * lanes))
+        small_vec = jnp.pad(small_vec, (0, small_rows * dp_count * lanes - small_len))
+        small_block = jnp.pad(
+            small_vec.reshape(dp_count, small_rows, lanes),
+            ((0, 0), (0, own_rows - small_rows), (0, 0)),
+        ).reshape(dp_count * own_rows, lanes)
+        joined, early_sum = lax.optimization_barrier(
+            (join_parts(parts + (small_block,)), early_sum)
+        )
+        last_sum = scatter_joined(joined)
+        qkv_sum, dense_sum, small_sum = split_cols(
+            last_sum.astype(jnp.float32), widths[:2] + [lanes]
+        )
+        up_sum, down_sum = split_cols(early_sum.astype(jnp.float32), widths[2:])
+    reduced = [(qkv_sum, dense_sum, up_sum, down_sum)] + [
+        split_cols(summed.astype(jnp.float32), widths) for summed in reduced[1:]
+    ]
+    qkv_grad = jnp.stack([reduced[layer_idx][0] for layer_idx in layer_ids])
+    dense_grad = jnp.stack([reduced[layer_idx][1] for layer_idx in layer_ids])
+    up_grad = jnp.stack([reduced[layer_idx][2] for layer_idx in layer_ids])
+    down_grad = jnp.stack([reduced[layer_idx][3] for layer_idx in layer_ids])
+    small_all = lax.all_gather(small_sum[:small_rows], ("dp", "mp"), axis=0, tiled=True)
+    small_all = jnp.transpose(
+        small_all.reshape(dp_count, mp_count, small_rows * lanes), (1, 0, 2)
+    ).reshape(mp_count, -1)
+    shared_len = shared_part.shape[0]
+    shared_sum = jnp.sum(small_all[:, :shared_len], axis=0).reshape((3,) + norm_gain.shape)
+    gain_grad, nbias_grad, obias_grad = shared_sum[0], shared_sum[1], shared_sum[2]
+    qbias_len = layer_count * qkv_cols
+    qbias_all = small_all[:, shared_len : shared_len + qbias_len]
+    ubias_all = small_all[:, shared_len + qbias_len : small_len]
+
+    def unfold(per_rank, width):
+        return jnp.transpose(
+            per_rank.reshape(mp_count, layer_count, width), (1, 0, 2)
+        ).reshape(layer_count, mp_count * width)
+
+    qbias_grad = unfold(qbias_all, qkv_cols)
+    ubias_grad = unfold(ubias_all, up_cols)
     qkv_new, qkv_states = adamw(w_qkv, qkv_grad, qkv_moments, weight_decay)
     dense_new, dense_states = adamw(w_dense, dense_grad, dense_moments, weight_decay)
     up_new, up_states = adamw(w_up, up_grad, up_moments, weight_decay)

time: 1490 us -> 822 us (0.55)
  waiting for transfers between devices: 1200 us -> 239 us
  Pallas kernels: 0 us -> 253 us
  local copies, waits for them, and re-layouts: 31.9 us -> 95.4 us
  blocking collectives: 65.8 us -> 43 us
    reduce_scatter x16 -> x0, waiting for transfers between devices: 727 us -> none  [the longest x2 131 us: per_device(): lax.psum_scatter(weight_grads[0].astype(jnp.bfloat16), 'dp', scatter_dime...]
    pallas_call x0 -> x16, Pallas kernels: none -> 253 us  [the longest x8 127 us: gather_rows(): pl.pallas_call(functools.partial(gather_kernel, count), out_shape=jax.Sha...]
    all_gather x14 -> x3, waiting for transfers between devices: 339 us -> 121 us  [gather_joined(): lax.all_gather(jnp.concatenate(pieces, axis=1), 'dp', axis=0, tiled=True)]
    psum x1 -> x0, waiting for transfers between devices: 128 us -> none  [per_device(): lax.psum((gain_part, nbias_part, qbias_part, obias_part, ubias_part), ('d...]
    unnamed x31 -> x9, waiting for transfers between devices: 2.35 us -> 119 us
    unnamed x187 -> x202, local copies, waits for them, and re-layouts: 23.4 us -> 69.1 us
    all_gather x2 -> x1, blocking collectives: 65.8 us -> 43 us  [per_device(): lax.all_gather(small_sum[:small_rows], ('dp', 'mp'), axis=0, tiled=True)]
  transfers between devices with their start and end apart: 31 -> 6, of which waited for: 29 -> 6; matrix products, arithmetic and copies ran while one was open for 7% -> 14% of each run, Pallas kernels for 0% -> 18%
where the time goes in v1:
time: 822 us; the launch traced here: 809 us
  Pallas kernels  253 us (31%)
  waiting for transfers between devices  239 us (29%)
  local copies, waits for them, and re-layouts  95.4 us (12%)
  matrix products  94.3 us (11%)
  other arithmetic  67.6 us (8%)
  blocking collectives  43 us (5%)
  between operations  16.3 us (2%)
    pallas_call x8, Pallas kernels, gather_rows(): pl.pallas_call(functools.partial(gather_kernel, count), out_shape=jax.Sha...  127 us
    pallas_call x8, Pallas kernels, scatter_rows(): pl.pallas_call(functools.partial(scatter_kernel, count), out_shape=jax.Sh...  127 us
    all_gather x3, waiting for transfers between devices, gather_joined(): lax.all_gather(jnp.concatenate(pieces, axis=1), 'dp', axis=0, tiled=True)  121 us
    unnamed x9, waiting for transfers between devices  119 us
    unnamed x202, local copies, waits for them, and re-layouts  69.1 us
    all_gather x1, blocking collectives, per_device(): lax.all_gather(small_sum[:small_rows], ('dp', 'mp'), axis=0, tiled=True)  43 us
    dot_general x8, matrix products, local_parts(): lax.dot_general(left_op, right_op, contract_rows, preferred_element_type=...  27.1 us
  transfers between devices with their start and end apart: 6, of which 6 were waited for; matrix products, arithmetic and copies ran while one was open for 14% of the time, Pallas kernels for 18%

profile of v1, /device:TPU:0, one launch (start us, length us, event | category | flops | bytes accessed | tf_op | source)
XLA Modules:
  0.0 809.4 jit_solution(5368360003628055322)
XLA Ops:
  14.0 16.8 %gather_rows.8 = bf16[512,1024]{1,0:T(8,128)(2,1)} custom-call(bf16[128,1024]{1,0:T(8,128)(2,1)} %add_convert_fusion.5.rows_ref), custom_call_target="tpu_custom_call" | custom-call | bytes 40000000 | tf_op jit(solution)/shard_map/gather_rows/pallas_call | solution.py:177
  33.0 29.6 %all-gather.4.cloned.1.call-done = bf16[1024,1024]{1,0:T(8,128)(2,1)} async-done(((bf16[128,1024]{1,0:T(8,128)(2,1)}), bf16[1024,1024]{1,0:T(8,128)(2,1)}) %all-gather.4.cloned.1.call-update) | async-done | bytes 2097168 | tf_op jit(solution)/shard_map/all_gather | solution.py:389
  72.1 15.5 %scatter_rows.8 = f32[128,1024]{1,0:T(8,128)} custom-call(bf16[512,1024]{1,0:T(8,128)(2,1)} %convolution_convert_fusion.8.parts_ref), custom_call_target="tpu_custom_call" | custom-call | bytes 40000000 | tf_op jit(solution)/shard_map/scatter_rows/pallas_call | solution.py:195
  89.9 16.0 %gather_rows.9 = bf16[512,1024]{1,0:T(8,128)(2,1)} custom-call(bf16[128,1024]{1,0:T(8,128)(2,1)} %add_convert_fusion.4.rows_ref), custom_call_target="tpu_custom_call" | custom-call | bytes 40000000 | tf_op jit(solution)/shard_map/gather_rows/pallas_call | solution.py:177
  105.9 30.7 %all-gather.6.cloned.1.call-done = bf16[1024,2048]{1,0:T(8,128)(2,1)} async-done(((bf16[128,2048]{1,0:T(8,128)(2,1)}), bf16[1024,2048]{1,0:T(8,128)(2,1)}) %all-gather.6.cloned.1.call-update) | async-done | bytes 4194320 | tf_op jit(solution)/shard_map/all_gather | solution.py:389
  142.4 15.4 %scatter_rows.9 = f32[128,1024]{1,0:T(8,128)} custom-call(bf16[512,1024]{1,0:T(8,128)(2,1)} %fusion.35.parts_ref), custom_call_target="tpu_custom_call" | custom-call | bytes 40000000 | tf_op jit(solution)/shard_map/scatter_rows/pallas_call | solution.py:195
  160.2 16.0 %gather_rows.10 = bf16[512,1024]{1,0:T(8,128)(2,1)} custom-call(bf16[128,1024]{1,0:T(8,128)(2,1)} %add_convert_fusion.3.rows_ref), custom_call_target="tpu_custom_call" | custom-call | bytes 40000000 | tf_op jit(solution)/shard_map/gather_rows/pallas_call | solution.py:177
  176.2 60.4 %all-gather.8.cloned.1.call-done = bf16[1024,3072]{1,0:T(8,128)(2,1)} async-done(((bf16[128,3072]{1,0:T(8,128)(2,1)}), bf16[1024,3072]{1,0:T(8,128)(2,1)}) %all-gather.8.cloned.1.call-update) | async-done | bytes 6291472 | tf_op jit(solution)/shard_map/all_gather | solution.py:389
  248.2 15.4 %scatter_rows.10 = f32[128,1024]{1,0:T(8,128)} custom-call(bf16[512,1024]{1,0:T(8,128)(2,1)} %convolution_convert_fusion.7.parts_ref), custom_call_target="tpu_custom_call" | custom-call | bytes 40000000 | tf_op jit(solution)/shard_map/scatter_rows/pallas_call | solution.py:195
  266.6 15.7 %gather_rows.11 = bf16[512,1024]{1,0:T(8,128)(2,1)} custom-call(bf16[128,1024]{1,0:T(8,128)(2,1)} %add_convert_fusion.2.rows_ref), custom_call_target="tpu_custom_call" | custom-call | bytes 40000000 | tf_op jit(solution)/shard_map/gather_rows/pallas_call | solution.py:177
  282.2 15.7 %gather_rows.12 = bf16[512,1024]{1,0:T(8,128)(2,1)} custom-call(bf16[128,1024]{1,0:T(8,128)(2,1)} %get-tuple-element.284.rows_ref), custom_call_target="tpu_custom_call" | custom-call | bytes 40000000 | tf_op jit(solution)/shard_map/gather_rows/pallas_call | solution.py:177
  301.2 4.7 fusion.144
  306.9 3.9 fusion.38.parts_ref
  310.7 15.8 %scatter_rows.12 = f32[128,1024]{1,0:T(8,128)} custom-call(bf16[512,1024]{1,0:T(8,128)(2,1)} %fusion.38.parts_ref), custom_call_target="tpu_custom_call" | custom-call | bytes 40000000 | tf_op jit(solution)/shard_map/scatter_rows/pallas_call | solution.py:195
  327.9 4.7 fusion.41.parts_ref
  332.6 15.9 %scatter_rows.11 = f32[128,1024]{1,0:T(8,128)} custom-call(bf16[512,1024]{1,0:T(8,128)(2,1)} %fusion.41.parts_ref), custom_call_target="tpu_custom_call" | custom-call | bytes 40000000 | tf_op jit(solution)/shard_map/scatter_rows/pallas_call | solution.py:195
  351.5 15.6 %gather_rows.13 = bf16[512,1024]{1,0:T(8,128)(2,1)} custom-call(bf16[128,1024]{1,0:T(8,128)(2,1)} %convert_element_type.238.rows_ref), custom_call_target="tpu_custom_call" | custom-call | bytes 40000000 | tf_op jit(solution)/shard_map/gather_rows/pallas_call | solution.py:177
  379.1 15.3 %convolution_convert_fusion.2 = bf16[1024,1024]{0,1:T(8,128)(2,1)} fusion(bf16[512,1024]{1,0:T(8,128)(2,1)S(1)} %copy-done.39, bf16[512,1024]{1,0:T(8,128)(2,1)S(1)} %copy-done.79), kind=kOutput, calls=%fused_computation.38 | convolution fusion | flops 1074790400 | bytes 4194304 | tf_op jit(solution)/shard_map/dot_general | solution.py:232
  402.4 15.8 %scatter_rows.13 = f32[128,1024]{1,0:T(8,128)} custom-call(bf16[512,1024]{1,0:T(8,128)(2,1)} %convolution_convert_fusion.6.parts_ref), custom_call_target="tpu_custom_call" | custom-call | bytes 40000000 | tf_op jit(solution)/shard_map/scatter_rows/pallas_call | solution.py:195
  421.0 5.4 pad_maximum_fusion
  426.4 8.6 %copy.261 = bf16[1024,3072]{1,0:T(8,128)(2,1)} copy(bf16[1024,3072]{0,1:T(8,128)(2,1)} %pad_maximum_fusion) | data formatting | bytes 12582912
  435.8 15.6 %gather_rows.14 = bf16[512,1024]{1,0:T(8,128)(2,1)} custom-call(bf16[128,1024]{1,0:T(8,128)(2,1)} %convert_element_type.251.rows_ref), custom_call_target="tpu_custom_call" | custom-call | bytes 40000000 | tf_op jit(solution)/shard_map/gather_rows/pallas_call | solution.py:177
  451.5 5.0 fusion.145
  459.8 16.3 %scatter_rows.14 = f32[128,1024]{1,0:T(8,128)} custom-call(bf16[512,1024]{1,0:T(8,128)(2,1)} %fusion.32.parts_ref), custom_call_target="tpu_custom_call" | custom-call | bytes 40000000 | tf_op jit(solution)/shard_map/scatter_rows/pallas_call | solution.py:195
  484.9 67.0 %reduce-scatter.10.cloned.1.call-done = bf16[128,3072]{1,0:T(8,128)(2,1)} async-done(((bf16[1024,3072]{1,0:T(8,128)(2,1)}), bf16[128,3072]{1,0:T(8,128)(2,1)}) %reduce-scatter.10.cloned.1.call-update) | async-done | bytes 786448
  554.2 6.5 copy.263
  561.5 15.2 %gather_rows.15 = bf16[512,1024]{1,0:T(8,128)(2,1)} custom-call(bf16[128,1024]{1,0:T(8,128)(2,1)} %convert_element_type.256.rows_ref), custom_call_target="tpu_custom_call" | custom-call | bytes 40000000 | tf_op jit(solution)/shard_map/gather_rows/pallas_call | solution.py:177
  589.2 16.4 %scatter_rows.15 = f32[128,1024]{1,0:T(8,128)} custom-call(bf16[512,1024]{1,0:T(8,128)(2,1)} %convolution_convert_fusion.5.parts_ref), custom_call_target="tpu_custom_call" | custom-call | bytes 40000000 | tf_op jit(solution)/shard_map/scatter_rows/pallas_call | solution.py:195
  615.9 32.5 %reduce-scatter.12.cloned.1.call-done = bf16[128,2048]{1,0:T(8,128)(2,1)} async-done(((bf16[1024,2048]{1,0:T(8,128)(2,1)}), bf16[128,2048]{1,0:T(8,128)(2,1)}) %reduce-scatter.12.cloned.1.call-update) | async-done | bytes 524304
  682.2 3.5 multiply_subtract_fusion
  703.4 19.0 %reduce-scatter.14.cloned.1.call-done = bf16[128,1152]{1,0:T(8,128)(2,1)} async-done(((bf16[1024,1152]{1,0:T(8,128)(2,1)}), bf16[128,1152]{1,0:T(8,128)(2,1)}) %reduce-scatter.14.cloned.1.call-update) | async-done | bytes 294928
  727.7 43.0 %all_gather.15 = f32[512,128]{1,0:T(8,128)} all-gather(f32[16,128]{1,0:T(8,128)S(1)} %copy.219), channel_id=1, replica_groups=mesh['dp'=8,'mp'=4] {'dp','mp'}, dimensions={0}, use_global_device_ids=true | all-gather | bytes 270336 | tf_op jit(solution)/shard_map/all_gather | solution.py:479
  (400 shorter events, 199.9 us)
Async XLA Ops:
  7.2 55.3 %all-gather.4.cloned.1.call-start = ((), (), s32[]{:S(2)}) async-start(), calls=%async_computation.3 | async-start | bytes 2359296 | tf_op jit(solution)/shard_map/all_gather | solution.py:389
  10.4 126.2 %all-gather.6.cloned.1.call-start = ((), (), s32[]{:S(2)}) async-start(), calls=%async_computation.4 | async-start | bytes 4718592 | tf_op jit(solution)/shard_map/all_gather | solution.py:389
  11.6 225.1 %all-gather.8.cloned.1.call-start = ((), (), s32[]{:S(2)}) async-start(), calls=%async_computation.5 | async-start | bytes 7077888 | tf_op jit(solution)/shard_map/all_gather | solution.py:389
  12.6 539.3 %reduce-scatter.10.cloned.1.call-start = ((), (), s32[]{:S(2)}) async-start(), calls=%async_computation.6 | async-start | bytes 7077888
  12.7 20.1 %copy-start.61 = (f32[2,2,1024]{2,1,0:T(2,128)S(1)}, f32[2,2,1024]{2,1,0:T(2,128)}, u32[]{:S(2)}) copy-start(f32[2,2,1024]{2,1,0:T(2,128)} %param.31) | copy-start | bytes 49156
  12.7 20.1 %copy-start.71 = (s32[1,512]{1,0:T(1,128)S(1)}, s32[1,512]{1,0:T(1,128)}, u32[]{:S(2)}) copy-start(s32[1,512]{1,0:T(1,128)} %param.22) | copy-start | bytes 6148
  32.7 32.8 %copy-start.44 = (f32[512,512]{0,1:T(8,128)}, f32[512,512]{0,1:T(8,128)S(1)}, u32[]{:S(2)}) copy-start(f32[512,512]{0,1:T(8,128)S(1)} %subtract_convert_fusion) | copy-start | bytes 3145732
  33.0 32.6 %copy-start.51 = (pred[512,512]{0,1:T(8,128)(4,1)}, pred[512,512]{0,1:T(8,128)(4,1)S(1)}, u32[]{:S(2)}) copy-start(pred[512,512]{0,1:T(8,128)(4,1)S(1)} %fusion.76) | copy-start | bytes 786436
  245.6 19.9 %copy-start.28 = (bf16[4,64,512]{2,1,0:T(8,128)(2,1)}, bf16[4,64,512]{2,1,0:T(8,128)(2,1)S(1)}, u32[]{:S(2)}) copy-start(bf16[4,64,512]{2,1,0:T(8,128)(2,1)S(1)} %convolution_convert_fusion.13) | copy-start | bytes 786436
  245.6 18.0 %copy-start.33 = (f32[128,1024]{1,0:T(8,128)S(1)}, f32[128,1024]{1,0:T(8,128)}, u32[]{:S(2)}) copy-start(f32[128,1024]{1,0:T(8,128)} %param.23) | copy-start | bytes 1572868
  301.2 4.7 copy-start.76
  327.9 20.7 %copy-start.8 = (f32[128,1024]{1,0:T(8,128)S(1)}, f32[128,1024]{1,0:T(8,128)}, u32[]{:S(2)}) copy-start(f32[128,1024]{1,0:T(8,128)} %scatter_rows.12) | copy-start | bytes 1572868
  350.8 16.4 %copy-start.29 = (bf16[4,64,512]{2,1,0:T(8,128)(2,1)S(1)}, bf16[4,64,512]{2,1,0:T(8,128)(2,1)}, u32[]{:S(2)}) copy-start(bf16[4,64,512]{2,1,0:T(8,128)(2,1)} %copy-done.28) | copy-start | bytes 786436
  374.5 21.1 %copy-start.9 = (f32[512,4,1,64]{0,3,1,2:T(8,128)}, f32[512,4,1,64]{0,3,1,2:T(8,128)S(1)}, u32[]{:S(2)}) copy-start(f32[512,4,1,64]{0,3,1,2:T(8,128)S(1)} %fusion.54) | copy-start | bytes 1572868
  376.1 19.5 %copy-start.11 = (f32[512,4,1,64]{0,3,1,2:T(8,128)}, f32[512,4,1,64]{0,3,1,2:T(8,128)S(1)}, u32[]{:S(2)}) copy-start(f32[512,4,1,64]{0,3,1,2:T(8,128)S(1)} %fusion.55) | copy-start | bytes 1572868
  379.1 15.3 %copy-start.19 = (bf16[512,1024]{1,0:T(8,128)(2,1)S(1)}, bf16[512,1024]{1,0:T(8,128)(2,1)}, u32[]{:S(2)}) copy-start(bf16[512,1024]{1,0:T(8,128)(2,1)} %gather_rows.13) | copy-start | bytes 3145732
  435.1 213.4 %reduce-scatter.12.cloned.1.call-start = ((), (), s32[]{:S(2)}) async-start(), calls=%async_computation.7 | async-start | bytes 4718592
  451.5 6.0 copy-start.73
  560.7 17.9 %copy-start.15 = (bf16[512,768]{0,1:T(8,128)(2,1)S(1)}, bf16[512,768]{0,1:T(8,128)(2,1)}, u32[]{:S(2)}) copy-start(bf16[512,768]{0,1:T(8,128)(2,1)} %copy-done.14) | copy-start | bytes 2359300
  560.7 161.6 %reduce-scatter.14.cloned.1.call-start = ((), (), s32[]{:S(2)}) async-start(), calls=%async_computation.8 | async-start | bytes 2654208
  703.4 73.4 %copy-start.7 = (f32[1,2,128,768]{2,3,1,0:T(8,128)S(1)}, f32[1,2,128,768]{2,3,1,0:T(8,128)}, u32[]{:S(2)}) copy-start(f32[1,2,128,768]{2,3,1,0:T(8,128)} %copy.273) | copy-start | bytes 2359300
  703.4 73.4 %copy-start.25 = (f32[2,128,768]{1,2,0:T(8,128)S(1)}, f32[2,128,768]{1,2,0:T(8,128)}, u32[]{:S(2)}) copy-start(f32[2,128,768]{1,2,0:T(8,128)} %copy.225) | copy-start | bytes 2359300
  703.4 73.4 %copy-start.34 = (f32[1,128,768]{1,2,0:T(8,128)S(1)}, f32[1,128,768]{1,2,0:T(8,128)}, u32[]{:S(2)}) copy-start(f32[1,128,768]{1,2,0:T(8,128)} %get-tuple-element.198) | copy-start | bytes 1179652
  776.8 5.0 copy-start.47
  779.5 8.5 %copy-start.26 = (f32[2,128,768]{1,2,0:T(8,128)S(1)}, f32[2,128,768]{1,2,0:T(8,128)}, u32[]{:S(2)}) copy-start(f32[2,128,768]{1,2,0:T(8,128)} %get-tuple-element.215) | copy-start | bytes 2359300
  781.9 9.1 %copy-start.35 = (f32[1,1,128,768]{2,3,1,0:T(8,128)S(1)}, f32[1,1,128,768]{2,3,1,0:T(8,128)}, u32[]{:S(2)}) copy-start(f32[1,1,128,768]{2,3,1,0:T(8,128)} %get-tuple-element.197) | copy-start | bytes 1179652
  786.4 10.5 %copy-start.63 = (f32[2,2,1024]{2,1,0:T(2,128)}, f32[2,2,1024]{2,1,0:T(2,128)S(1)}, u32[]{:S(2)}) copy-start(f32[2,2,1024]{2,1,0:T(2,128)S(1)} %slice.347) | copy-start | bytes 49156
  786.4 11.1 %copy-start.64 = (f32[2,2,1024]{2,1,0:T(2,128)}, f32[2,2,1024]{2,1,0:T(2,128)S(1)}, u32[]{:S(2)}) copy-start(f32[2,2,1024]{2,1,0:T(2,128)S(1)} %slice.349) | copy-start | bytes 49156
  787.2 8.0 copy-start.57
  787.2 11.0 %copy-start.65 = (f32[2,2,1024]{2,1,0:T(2,128)}, f32[2,2,1024]{2,1,0:T(2,128)S(1)}, u32[]{:S(2)}) copy-start(f32[2,2,1024]{2,1,0:T(2,128)S(1)} %slice.352) | copy-start | bytes 49156
  788.0 8.0 copy-start.56
  794.0 4.2 copy-start.62
  (56 other events, 130.1 us)
Sparse Core Ops, SparseCore 0:
  10.7 51.7 all-gather.3
  65.3 71.3 all-gather.5
  139.4 97.2 all-gather.7
  435.2 116.6 reduce-scatter.9
  560.9 87.5 reduce-scatter.11
  653.2 69.1 reduce-scatter.13
